TPU v7x, 32 devices: a whole 2x2x4 slice. The times are simulated.
32 devices in a mesh: chan: 8 (over z, y), tm: 4 (over x, core).
Axes of the slice: x: 2, y: 2, z: 4, core: 2. Of those that a mesh axis runs over, the one named last changes fastest.
Arguments:
- record: bfloat16 [96, 2048], P('chan', 'tm'), may hold values from -6 to 6
- fir: float32 [96, 65], P('chan'), may hold values from -0.75 to 0.75
Outputs:
- xcorr: float32 [4, 96, 96, 256], P('tm', 'chan')
All inputs are finite; a program needn't handle non-finite values.
Results may differ from a plain program's by a relative error of at most 0.004.
Values may be sent and summed in bfloat16 or wider, within the bound.
A program may use at most 64 MiB of HBM per device.

v0:
```python
import math
import jax
import jax.numpy as jnp
from jax import lax
from jax.sharding import PartitionSpec as P

GROUP = 512
MAXLAG = 128


def extended_2(block, sides, width):
    for axis, dim in sides:
        count = lax.axis_size(axis)
        forward = [(i, i + 1) for i in range(count - 1)]
        backward = [(target, source) for source, target in forward]
        low = lax.ppermute(
            lax.slice_in_dim(block, block.shape[dim] - width, None, axis=dim), axis, forward
        )
        high = lax.ppermute(lax.slice_in_dim(block, 0, width, axis=dim), axis, backward)
        block = jnp.concatenate([low, block, high], axis=dim)
    return block


def whiten(widened_raw, fir, length):
    widened = widened_raw.astype(jnp.float32)
    running = jnp.zeros((widened.shape[0], length), jnp.float32)
    for k in range(fir.shape[1]):
        running = running + fir[:, k : k + 1] * widened[:, k : k + length]
    return running


def local(record, fir):
    ch_dev = record.shape[0]
    local_len = record.shape[1]
    half_width = (fir.shape[1] - 1) // 2
    lag_count = 2 * MAXLAG
    span = GROUP + lag_count
    factor = 1.0 / math.sqrt(GROUP)
    raw_ext = extended_2(record, (("tm", 1),), half_width)
    whitened = whiten(raw_ext, fir, local_len).astype(jnp.bfloat16)
    extended = extended_2(whitened, (("tm", 1),), MAXLAG)
    c = 0
    segment = extended[:, c * GROUP + MAXLAG : c * GROUP + MAXLAG + GROUP]
    padded = jnp.concatenate([segment, jnp.zeros((ch_dev, lag_count + 1), jnp.bfloat16)], axis=1)
    tiled = jnp.tile(padded, (1, lag_count))[:, : lag_count * span]
    expanded = [tiled.reshape(ch_dev, lag_count, span)]
    c = 0
    window = lax.all_gather(extended, "chan", axis=0, tiled=True)
    blocks = [
        jnp.einsum("amu,ju->ajm", expanded[c], window, preferred_element_type=jnp.float32) * factor
    ]
    return jnp.stack(blocks)


def solution(mesh):
    in_specs = (P("chan", "tm"), P("chan", None))
    out_specs = P("tm", "chan", None, None)
    return jax.shard_map(local, mesh=mesh, in_specs=in_specs, out_specs=out_specs, check_vma=False)
```

profile of v0, /device:TPU:6, one launch (start us, length us, event | category | flops | bytes accessed | tf_op | source)
XLA Modules:
  0.0 80.0 jit_solution(231138366995109417)
XLA Ops:
  0.0 0.8 fusion.74
  0.8 1.9 %collective-permute-start = (bf16[12,32]{1,0:T(8,128)(2,1)S(1)}, bf16[12,32]{1,0:T(8,128)(2,1)S(1)}, u32[]{:S(2)}, u32[]{:S(2)}) collective-permute-start(bf16[12,32]{1,0:T(8,128)(2,1)S(1)} %get-tuple-element.72), channel_id=1, source_target_pairs={{0,1},{1,2},{2,3},{4,5},{5,6},{6,7},{8,9},{9,10},{10,11},{12,13},{... | collective-permute-start | bytes 2312 | tf_op jit(solution)/shard_map/ppermute | solution.py:16
  2.7 3.6 %collective-permute-start.1 = (bf16[12,32]{1,0:T(8,128)(2,1)S(1)}, bf16[12,32]{1,0:T(8,128)(2,1)S(1)}, u32[]{:S(2)}, u32[]{:S(2)}) collective-permute-start(bf16[12,32]{1,0:T(8,128)(2,1)S(1)} %get-tuple-element.73), channel_id=1, source_target_pairs={{1,0},{2,1},{3,2},{5,4},{6,5},{7,6},{9,8},{10,9},{11,10},{13,12},{... | collective-permute-start | bytes 2312 | tf_op jit(solution)/shard_map/ppermute | solution.py:19
  6.3 1.9 %slice_reduce_fusion.64 = (f32[12]{0:T(128)S(1)}, f32[12]{0:T(128)S(1)}, f32[12]{0:T(128)S(1)}, f32[12]{0:T(128)S(1)}, f32[12]{0:T(128)S(1)}, /*index=5*/f32[12]...) fusion(f32[12,65]{1,0:T(8,128)} %param.3), kind=kLoop, calls=%fused_computation.200 | loop fusion | bytes 1824 | tf_op jit(solution)/shard_map/slice | solution.py:28
  8.3 1.9 %slice_reduce_fusion.63 = (f32[12]{0:T(128)S(1)}, f32[12]{0:T(128)S(1)}, f32[12]{0:T(128)S(1)}, f32[12]{0:T(128)S(1)}, f32[12]{0:T(128)S(1)}, /*index=5*/f32[12]...) fusion(f32[12,65]{1,0:T(8,128)} %param.3), kind=kLoop, calls=%fused_computation.199 | loop fusion | bytes 1824 | tf_op jit(solution)/shard_map/slice | solution.py:28
  10.2 1.9 %slice_reduce_fusion.62 = (f32[12]{0:T(128)S(1)}, f32[12]{0:T(128)S(1)}, f32[12]{0:T(128)S(1)}, f32[12]{0:T(128)S(1)}, f32[12]{0:T(128)S(1)}, /*index=5*/f32[12]...) fusion(f32[12,65]{1,0:T(8,128)} %param.3), kind=kLoop, calls=%fused_computation.198 | loop fusion | bytes 1824 | tf_op jit(solution)/shard_map/slice | solution.py:28
  12.1 1.3 %slice_reduce_fusion.61 = (f32[12]{0:T(128)S(1)}, f32[12]{0:T(128)S(1)}, f32[12]{0:T(128)S(1)}, f32[12]{0:T(128)S(1)}, f32[12]{0:T(128)S(1)}, /*index=5*/f32[12]{0:T(128)S(1)}, f32[12]{0:T(128)S(1)}, f32[12]{0:T(128)S(1)}) fusion(f32[12,65]{1,0:T(8,128)} %param.3), kind=kLoop, calls=%fused_computation.197 | loop fusion | bytes 768 | tf_op jit(solution)/shard_map/slice | solution.py:28
  13.4 0.0 collective-permute-done
  13.5 0.0 collective-permute-done.1
  13.5 0.8 maximum_convert_fusion
  14.3 0.8 fusion.9
  15.1 1.9 %collective-permute-start.2 = (bf16[12,128]{1,0:T(8,128)(2,1)S(1)}, bf16[12,128]{1,0:T(8,128)(2,1)S(1)}, u32[]{:S(2)}, u32[]{:S(2)}) collective-permute-start(bf16[12,128]{1,0:T(8,128)(2,1)S(1)} %get-tuple-element.70), channel_id=1, source_target_pairs={{0,1},{1,2},{2,3},{4,5},{5,6},{6,7},{8,9},{9,10},{10,11},{12,13},{... | collective-permute-start | bytes 9224 | tf_op jit(solution)/shard_map/ppermute | solution.py:16
  17.0 3.6 %collective-permute-start.3 = (bf16[12,128]{1,0:T(8,128)(2,1)S(1)}, bf16[12,128]{1,0:T(8,128)(2,1)S(1)}, u32[]{:S(2)}, u32[]{:S(2)}) collective-permute-start(bf16[12,128]{1,0:T(8,128)(2,1)S(1)} %get-tuple-element.71), channel_id=1, source_target_pairs={{1,0},{2,1},{3,2},{5,4},{6,5},{7,6},{9,8},{10,9},{11,10},{13,12},{... | collective-permute-start | bytes 9224 | tf_op jit(solution)/shard_map/ppermute | solution.py:19
  20.7 2.9 %tile.4 = bf16[12,256,769]{2,1,0:T(8,128)(2,1)} broadcast(bf16[12,769]{1,0:T(8,128)(2,1)S(1)} %concatenate.11), dimensions={0,2} | broadcast | bytes 4743192 | tf_op jit(solution)/shard_map/tile | solution.py:45
  23.5 13.6 %tile.10 = bf16[12,196864]{1,0:T(8,128)(2,1)} reshape(bf16[12,256,769]{2,1,0:T(8,128)(2,1)} %tile.4) | data formatting | bytes 9449472 | tf_op jit(solution)/shard_map/tile | solution.py:45
  37.1 0.0 slice-start
  37.1 2.8 %slice-done = bf16[12,196608]{1,0:T(8,128)(2,1)S(1)} async-done(((bf16[12,196864]{1,0:T(8,128)(2,1)}), bf16[12,196608]{1,0:T(8,128)(2,1)S(1)}, s32[]{:S(2)}) %slice-start) | async-done | bytes 4718616 | tf_op jit(solution)/shard_map/slice | solution.py:45
  39.9 4.1 %copy.3 = bf16[2,8,256,768]{3,2,1,0:T(8,128)(2,1)} copy(bf16[2,8,256,768]{3,1,2,0:T(8,128)(2,1)S(1)} %bitcast.10) | data formatting | bytes 12582912
  44.0 0.0 collective-permute-done.2
  44.0 0.0 collective-permute-done.3
  44.0 31.0 %all-gather = bf16[8,12,768]{2,1,0:T(8,128)(2,1)S(1)} all-gather(bf16[1,12,768]{2,1,0:T(8,128)(2,1)S(1)} %maximum_bitcast_fusion), channel_id=1, replica_groups=mesh['chan'=8,'tm'=4] {'chan'}, dimensions={0}, use_global_device_ids=true | all-gather | bytes 165888 | tf_op jit(solution)/shard_map/all_gather | solution.py:48
  75.1 4.9 %fusion.5 = f32[1,12,96,256]{3,2,1,0:T(8,128)} fusion(bf16[96,768,1]{1,0,2:T(8,128)(2,1)S(1)} %reshape.10, bf16[16,256,768]{2,1,0:T(8,128)(2,1)} %bitcast.11), kind=kOutput, calls=%fused_computation.3 | convolution fusion | flops 453279744 | bytes 6045696 | tf_op jit(solution)/shard_map/amu,ju->ajm/dot_general | solution.py:50
  (4 shorter events, 0.1 us)
Async XLA Ops:
  0.8 12.7 %collective-permute-start = (bf16[12,32]{1,0:T(8,128)(2,1)S(1)}, bf16[12,32]{1,0:T(8,128)(2,1)S(1)}, u32[]{:S(2)}, u32[]{:S(2)}) collective-permute-start(bf16[12,32]{1,0:T(8,128)(2,1)S(1)} %get-tuple-element.72), channel_id=1, source_target_pairs={{0,1},{1,2},{2,3},{4,5},{5,6},{6,7},{8,9},{9,10},{10,11},{12,13},{... | collective-permute-start | bytes 2312 | tf_op jit(solution)/shard_map/ppermute | solution.py:16
  2.7 10.8 %collective-permute-start.1 = (bf16[12,32]{1,0:T(8,128)(2,1)S(1)}, bf16[12,32]{1,0:T(8,128)(2,1)S(1)}, u32[]{:S(2)}, u32[]{:S(2)}) collective-permute-start(bf16[12,32]{1,0:T(8,128)(2,1)S(1)} %get-tuple-element.73), channel_id=1, source_target_pairs={{1,0},{2,1},{3,2},{5,4},{6,5},{7,6},{9,8},{10,9},{11,10},{13,12},{... | collective-permute-start | bytes 2312 | tf_op jit(solution)/shard_map/ppermute | solution.py:19
  15.1 28.9 %collective-permute-start.2 = (bf16[12,128]{1,0:T(8,128)(2,1)S(1)}, bf16[12,128]{1,0:T(8,128)(2,1)S(1)}, u32[]{:S(2)}, u32[]{:S(2)}) collective-permute-start(bf16[12,128]{1,0:T(8,128)(2,1)S(1)} %get-tuple-element.70), channel_id=1, source_target_pairs={{0,1},{1,2},{2,3},{4,5},{5,6},{6,7},{8,9},{9,10},{10,11},{12,13},{... | collective-permute-start | bytes 9224 | tf_op jit(solution)/shard_map/ppermute | solution.py:16
  17.0 27.0 %collective-permute-start.3 = (bf16[12,128]{1,0:T(8,128)(2,1)S(1)}, bf16[12,128]{1,0:T(8,128)(2,1)S(1)}, u32[]{:S(2)}, u32[]{:S(2)}) collective-permute-start(bf16[12,128]{1,0:T(8,128)(2,1)S(1)} %get-tuple-element.71), channel_id=1, source_target_pairs={{1,0},{2,1},{3,2},{5,4},{6,5},{7,6},{9,8},{10,9},{11,10},{13,12},{... | collective-permute-start | bytes 9224 | tf_op jit(solution)/shard_map/ppermute | solution.py:19
  37.1 2.8 %slice-start = ((bf16[12,196864]{1,0:T(8,128)(2,1)}), bf16[12,196608]{1,0:T(8,128)(2,1)S(1)}, s32[]{:S(2)}) async-start(bf16[12,196864]{1,0:T(8,128)(2,1)} %tile.10), calls=%async_computation | async-start | bytes 12582912 | tf_op jit(solution)/shard_map/slice | solution.py:45
where the time goes:
time: 80.6 us; the launch traced here: 80 us
  local copies, waits for them, and re-layouts  31.2 us (39%)
  blocking collectives  31 us (38%)
  starting transfers between devices  11.1 us (14%)
  matrix products  4.89 us (6%)
  other arithmetic  1.59 us (2%)
    all_gather x1, blocking collectives, local(): window = lax.all_gather(extended, 'chan', axis=0, tiled=True)  31 us
    another operation x2, local copies, waits for them, and re-layouts, local(): tiled = jnp.tile(padded, (1, lag_count))[:, :lag_count * span]  16.5 us
    ppermute x2, starting transfers between devices, extended_2(): lax.ppermute(lax.slice_in_dim(block, 0, width, axis=dim), axis, backward)  7.28 us
    slice x4, local copies, waits for them, and re-layouts, whiten(): running = running + fir[:, k:k + 1] * widened[:, k:k + length]  7.1 us
    dot_general x1, matrix products, local(): jnp.einsum('amu,ju->ajm', expanded[c], window, preferred_element_type=jnp...  4.89 us
    unnamed x2, local copies, waits for them, and re-layouts  4.09 us
    ppermute x2, starting transfers between devices, extended_2(): lax.ppermute(lax.slice_in_dim(block, block.shape[dim] - width, None, axis...  3.83 us
    slice x2, local copies, waits for them, and re-layouts, local(): tiled = jnp.tile(padded, (1, lag_count))[:, :lag_count * span]  2.78 us
  transfers between devices with their start and end apart: 4, of which 0 were waited for; matrix products, arithmetic and copies ran while one was open for 35% of the time, Pallas kernels for 0%

commit v1 on v0

--- a/solution.py
+++ b/solution.py
@@ -6,6 +6,18 @@
 
 GROUP = 512
 MAXLAG = 128
+
+
+def collect(x, axis, dim):
+    ways, here = (lax.axis_size(axis), lax.axis_index(axis))
+    grown, reach = (x, 1)
+    while reach < ways:
+        theirs = lax.ppermute(grown, axis, [(d, d ^ reach) for d in range(ways)])
+        mine_first = jnp.concatenate([grown, theirs], axis=dim)
+        theirs_first = jnp.concatenate([theirs, grown], axis=dim)
+        grown = jnp.where(here & reach == 0, mine_first, theirs_first)
+        reach = 2 * reach
+    return grown
 
 
 def extended_2(block, sides, width):
@@ -45,7 +57,7 @@
     tiled = jnp.tile(padded, (1, lag_count))[:, : lag_count * span]
     expanded = [tiled.reshape(ch_dev, lag_count, span)]
     c = 0
-    window = lax.all_gather(extended, "chan", axis=0, tiled=True)
+    window = collect(extended, "chan", 0)
     blocks = [
         jnp.einsum("amu,ju->ajm", expanded[c], window, preferred_element_type=jnp.float32) * factor
     ]

time: 80.6 us -> 57.2 us (0.71)
  the two profiles are of different devices: /device:TPU:6 before, /device:TPU:0 now
where the time goes in v1:
time: 57.2 us; the launch traced here: 56.5 us
  local copies, waits for them, and re-layouts  28.5 us (50%)
  starting transfers between devices  15.9 us (28%)
  waiting for transfers between devices  7.84 us (14%)
  matrix products  2.57 us (4%)
  other arithmetic  1.63 us (3%)
    another operation x2, local copies, waits for them, and re-layouts, local(): tiled = jnp.tile(padded, (1, lag_count))[:, :lag_count * span]  16.5 us
    ppermute x2, starting transfers between devices, extended_2(): lax.ppermute(lax.slice_in_dim(block, block.shape[dim] - width, None, axis...  7.48 us
    slice x4, local copies, waits for them, and re-layouts, whiten(): running = running + fir[:, k:k + 1] * widened[:, k:k + length]  7.1 us
    ppermute x3, starting transfers between devices, collect(): theirs = lax.ppermute(grown, axis, [(d, d ^ reach) for d in range(ways)])  5.82 us
    ppermute x3, waiting for transfers between devices, collect(): theirs = lax.ppermute(grown, axis, [(d, d ^ reach) for d in range(ways)])  4.84 us
    ppermute x2, waiting for transfers between devices, extended_2(): lax.ppermute(lax.slice_in_dim(block, 0, width, axis=dim), axis, backward)  2.99 us
    slice x2, local copies, waits for them, and re-layouts, local(): tiled = jnp.tile(padded, (1, lag_count))[:, :lag_count * span]  2.78 us
    ppermute x2, starting transfers between devices, extended_2(): lax.ppermute(lax.slice_in_dim(block, 0, width, axis=dim), axis, backward)  2.58 us
  transfers between devices with their start and end apart: 7, of which 3 were waited for; matrix products, arithmetic and copies ran while one was open for 44% of the time, Pallas kernels for 0%

profile of v1, /device:TPU:0, one launch (start us, length us, event | category | flops | bytes accessed | tf_op | source)
XLA Modules:
  0.0 56.5 jit_solution(5282772845729023448)
XLA Ops:
  0.0 0.8 %fusion.83 = (bf16[12,32]{1,0:T(8,128)(2,1)S(1)}, bf16[12,32]{1,0:T(8,128)(2,1)S(1)}) fusion(bf16[12,512]{1,0:T(8,128)(2,1)} %param.2), kind=kLoop, calls=%fused_computation.213 | loop fusion | bytes 3072 | tf_op jit(solution)/shard_map/slice | solution.py:29
  0.8 2.3 %collective-permute-start = (bf16[12,32]{1,0:T(8,128)(2,1)S(1)}, bf16[12,32]{1,0:T(8,128)(2,1)S(1)}, u32[]{:S(2)}, u32[]{:S(2)}) collective-permute-start(bf16[12,32]{1,0:T(8,128)(2,1)S(1)} %get-tuple-element.72), channel_id=1, source_target_pairs={{0,1},{1,2},{2,3},{4,5},{5,6},{6,7},{8,9},{9,10},{10,11},{12,13},{... | collective-permute-start | bytes 2312 | tf_op jit(solution)/shard_map/ppermute | solution.py:28
  3.1 1.3 %collective-permute-start.1 = (bf16[12,32]{1,0:T(8,128)(2,1)S(1)}, bf16[12,32]{1,0:T(8,128)(2,1)S(1)}, u32[]{:S(2)}, u32[]{:S(2)}) collective-permute-start(bf16[12,32]{1,0:T(8,128)(2,1)S(1)} %get-tuple-element.73), channel_id=1, source_target_pairs={{1,0},{2,1},{3,2},{5,4},{6,5},{7,6},{9,8},{10,9},{11,10},{13,12},{... | collective-permute-start | bytes 2312 | tf_op jit(solution)/shard_map/ppermute | solution.py:31
  4.4 1.9 %slice_reduce_fusion.64 = (f32[12]{0:T(128)S(1)}, f32[12]{0:T(128)S(1)}, f32[12]{0:T(128)S(1)}, f32[12]{0:T(128)S(1)}, f32[12]{0:T(128)S(1)}, /*index=5*/f32[12]...) fusion(f32[12,65]{1,0:T(8,128)} %param.3), kind=kLoop, calls=%fused_computation.210 | loop fusion | bytes 1824 | tf_op jit(solution)/shard_map/slice | solution.py:40
  6.4 1.9 %slice_reduce_fusion.63 = (f32[12]{0:T(128)S(1)}, f32[12]{0:T(128)S(1)}, f32[12]{0:T(128)S(1)}, f32[12]{0:T(128)S(1)}, f32[12]{0:T(128)S(1)}, /*index=5*/f32[12]...) fusion(f32[12,65]{1,0:T(8,128)} %param.3), kind=kLoop, calls=%fused_computation.209 | loop fusion | bytes 1824 | tf_op jit(solution)/shard_map/slice | solution.py:40
  8.3 1.9 %slice_reduce_fusion.62 = (f32[12]{0:T(128)S(1)}, f32[12]{0:T(128)S(1)}, f32[12]{0:T(128)S(1)}, f32[12]{0:T(128)S(1)}, f32[12]{0:T(128)S(1)}, /*index=5*/f32[12]...) fusion(f32[12,65]{1,0:T(8,128)} %param.3), kind=kLoop, calls=%fused_computation.208 | loop fusion | bytes 1824 | tf_op jit(solution)/shard_map/slice | solution.py:40
  10.2 1.3 %slice_reduce_fusion.61 = (f32[12]{0:T(128)S(1)}, f32[12]{0:T(128)S(1)}, f32[12]{0:T(128)S(1)}, f32[12]{0:T(128)S(1)}, f32[12]{0:T(128)S(1)}, /*index=5*/f32[12]{0:T(128)S(1)}, f32[12]{0:T(128)S(1)}, f32[12]{0:T(128)S(1)}) fusion(f32[12,65]{1,0:T(8,128)} %param.3), kind=kLoop, calls=%fused_computation.207 | loop fusion | bytes 768 | tf_op jit(solution)/shard_map/slice | solution.py:40
  11.5 0.0 collective-permute-done
  11.5 0.0 collective-permute-done.1
  11.6 0.8 %maximum_convert_fusion = f32[12,576]{1,0:T(8,128)S(1)} fusion(bf16[12,32]{1,0:T(8,128)(2,1)S(1)} %collective-permute-done.1, bf16[12,512]{1,0:T(8,128)(2,1)} %param.2, bf16[12,32]{1,0:T(8,128)(2,1)S(1)} %collective-permute-done), kind=kLoop, calls=%fused_computation.145 | loop fusion | flops 41472 | bytes 41472 | tf_op jit(solution)/shard_map/convert_element_type | solution.py:37
  12.3 0.8 %fusion.17 = bf16[12,512]{1,0:T(8,128)(2,1)S(1)} fusion(f32[12,576]{1,0:T(8,128)S(1)} %maximum_convert_fusion, f32[12]{0:T(128)S(1)} %get-tuple-element.68, f32[12]{0:T(128)S(1)} %get-tuple-element.69, f32[12]{0:T(128)S(1)} %get-tuple-element.6, f32[12]{0:T(128)S(1)} %get-tuple-element.7, f32[12]{0:T(128)S(1)} %get-tuple-element.8, ...), kind=kLoop, calls=%fused_computation.16 | loop fusion | flops 798720 | bytes 1612848 | tf_op jit(solution)/shard_map/convert_element_type | solution.py:52
  13.2 5.1 %collective-permute-start.2 = (bf16[12,128]{1,0:T(8,128)(2,1)S(1)}, bf16[12,128]{1,0:T(8,128)(2,1)S(1)}, u32[]{:S(2)}, u32[]{:S(2)}) collective-permute-start(bf16[12,128]{1,0:T(8,128)(2,1)S(1)} %get-tuple-element.70), channel_id=1, source_target_pairs={{0,1},{1,2},{2,3},{4,5},{5,6},{6,7},{8,9},{9,10},{10,11},{12,13},{... | collective-permute-start | bytes 9224 | tf_op jit(solution)/shard_map/ppermute | solution.py:28
  18.3 1.3 %collective-permute-start.3 = (bf16[12,128]{1,0:T(8,128)(2,1)S(1)}, bf16[12,128]{1,0:T(8,128)(2,1)S(1)}, u32[]{:S(2)}, u32[]{:S(2)}) collective-permute-start(bf16[12,128]{1,0:T(8,128)(2,1)S(1)} %get-tuple-element.71), channel_id=1, source_target_pairs={{1,0},{2,1},{3,2},{5,4},{6,5},{7,6},{9,8},{10,9},{11,10},{13,12},{... | collective-permute-start | bytes 9224 | tf_op jit(solution)/shard_map/ppermute | solution.py:31
  19.6 0.0 collective-permute-done.2
  19.6 3.0 %collective-permute-done.3 = bf16[12,128]{1,0:T(8,128)(2,1)S(1)} collective-permute-done((bf16[12,128]{1,0:T(8,128)(2,1)S(1)}, bf16[12,128]{1,0:T(8,128)(2,1)S(1)}, u32[]{:S(2)}, u32[]{:S(2)}) %collective-permute-start.3) | collective-permute-done | bytes 3104 | tf_op jit(solution)/shard_map/ppermute | solution.py:31
  22.6 1.5 %collective-permute-start.4 = (bf16[12,768]{1,0:T(8,128)(2,1)S(1)}, bf16[12,768]{1,0:T(8,128)(2,1)S(1)}, u32[]{:S(2)}, u32[]{:S(2)}) collective-permute-start(bf16[12,768]{1,0:T(8,128)(2,1)S(1)} %pad_maximum_fusion), channel_id=1, source_target_pairs={{0,4},{4,0},{8,12},{12,8},{16,20},{20,16},{24,28},{28,24},{1,5},{5... | collective-permute-start | bytes 55304 | tf_op jit(solution)/shard_map/ppermute | solution.py:15
  24.1 2.3 %collective-permute-done.4 = bf16[12,768]{1,0:T(8,128)(2,1)S(1)} collective-permute-done((bf16[12,768]{1,0:T(8,128)(2,1)S(1)}, bf16[12,768]{1,0:T(8,128)(2,1)S(1)}, u32[]{:S(2)}, u32[]{:S(2)}) %collective-permute-start.4) | collective-permute-done | bytes 18464 | tf_op jit(solution)/shard_map/ppermute | solution.py:15
  26.5 1.6 %collective-permute-start.5 = (bf16[24,768]{1,0:T(8,128)(2,1)S(1)}, bf16[24,768]{1,0:T(8,128)(2,1)S(1)}, u32[]{:S(2)}, u32[]{:S(2)}) collective-permute-start(bf16[24,768]{1,0:T(8,128)(2,1)S(1)} %maximum_select_fusion.2), channel_id=1, source_target_pairs={{0,8},{4,12},{8,0},{12,4},{16,24},{20,28},{24,16},{28,20},{1,9},{5... | collective-permute-start | bytes 110600 | tf_op jit(solution)/shard_map/ppermute | solution.py:15
  28.1 2.5 %collective-permute-done.5 = bf16[24,768]{1,0:T(8,128)(2,1)S(1)} collective-permute-done((bf16[24,768]{1,0:T(8,128)(2,1)S(1)}, bf16[24,768]{1,0:T(8,128)(2,1)S(1)}, u32[]{:S(2)}, u32[]{:S(2)}) %collective-permute-start.5) | collective-permute-done | bytes 36896 | tf_op jit(solution)/shard_map/ppermute | solution.py:15
  30.7 2.7 %collective-permute-start.6 = (bf16[48,768]{1,0:T(8,128)(2,1)S(1)}, bf16[48,768]{1,0:T(8,128)(2,1)S(1)}, u32[]{:S(2)}, u32[]{:S(2)}) collective-permute-start(bf16[48,768]{1,0:T(8,128)(2,1)S(1)} %maximum_select_fusion.1), channel_id=1, source_target_pairs={{0,16},{4,20},{8,24},{12,28},{16,0},{20,4},{24,8},{28,12},{1,17},{... | collective-permute-start | bytes 221192 | tf_op jit(solution)/shard_map/ppermute | solution.py:15
  33.3 2.9 %tile.4 = bf16[12,256,769]{2,1,0:T(8,128)(2,1)} broadcast(bf16[12,769]{1,0:T(8,128)(2,1)S(1)} %concatenate.35), dimensions={0,2} | broadcast | bytes 4743192 | tf_op jit(solution)/shard_map/tile | solution.py:57
  36.2 13.6 %tile.10 = bf16[12,196864]{1,0:T(8,128)(2,1)} reshape(bf16[12,256,769]{2,1,0:T(8,128)(2,1)} %tile.4) | data formatting | bytes 9449472 | tf_op jit(solution)/shard_map/tile | solution.py:57
  49.8 0.0 slice-start
  49.8 2.8 %slice-done = bf16[12,196608]{1,0:T(8,128)(2,1)S(1)} async-done(((bf16[12,196864]{1,0:T(8,128)(2,1)}), bf16[12,196608]{1,0:T(8,128)(2,1)S(1)}, s32[]{:S(2)}) %slice-start) | async-done | bytes 4718616 | tf_op jit(solution)/shard_map/slice | solution.py:57
  52.6 1.4 %copy.3 = bf16[2,8,256,768]{3,2,1,0:T(8,128)(2,1)S(1)} copy(bf16[2,8,256,768]{3,1,2,0:T(8,128)(2,1)S(1)} %bitcast.10) | data formatting | bytes 12582912
  54.0 0.0 collective-permute-done.6
  54.0 2.6 %fusion.5 = f32[1,12,96,256]{3,2,1,0:T(8,128)} fusion(bf16[16,256,768]{2,1,0:T(8,128)(2,1)S(1)} %bitcast.11, bf16[48,768]{1,0:T(8,128)(2,1)S(1)} %collective-permute-done.6, bf16[48,768]{1,0:T(8,128)(2,1)S(1)} %maximum_select_fusion.1, pred[]{:T(512)S(6)} %eq.9), kind=kOutput, calls=%fused_computation.3 | convolution fusion | flops 453943296 | bytes 6045697 | tf_op jit(solution)/shard_map/amu,ju->ajm/dot_general | solution.py:62
  (5 shorter events, 0.1 us)
Async XLA Ops:
  0.8 10.8 %collective-permute-start = (bf16[12,32]{1,0:T(8,128)(2,1)S(1)}, bf16[12,32]{1,0:T(8,128)(2,1)S(1)}, u32[]{:S(2)}, u32[]{:S(2)}) collective-permute-start(bf16[12,32]{1,0:T(8,128)(2,1)S(1)} %get-tuple-element.72), channel_id=1, source_target_pairs={{0,1},{1,2},{2,3},{4,5},{5,6},{6,7},{8,9},{9,10},{10,11},{12,13},{... | collective-permute-start | bytes 2312 | tf_op jit(solution)/shard_map/ppermute | solution.py:28
  3.1 8.4 %collective-permute-start.1 = (bf16[12,32]{1,0:T(8,128)(2,1)S(1)}, bf16[12,32]{1,0:T(8,128)(2,1)S(1)}, u32[]{:S(2)}, u32[]{:S(2)}) collective-permute-start(bf16[12,32]{1,0:T(8,128)(2,1)S(1)} %get-tuple-element.73), channel_id=1, source_target_pairs={{1,0},{2,1},{3,2},{5,4},{6,5},{7,6},{9,8},{10,9},{11,10},{13,12},{... | collective-permute-start | bytes 2312 | tf_op jit(solution)/shard_map/ppermute | solution.py:31
  13.2 6.4 %collective-permute-start.2 = (bf16[12,128]{1,0:T(8,128)(2,1)S(1)}, bf16[12,128]{1,0:T(8,128)(2,1)S(1)}, u32[]{:S(2)}, u32[]{:S(2)}) collective-permute-start(bf16[12,128]{1,0:T(8,128)(2,1)S(1)} %get-tuple-element.70), channel_id=1, source_target_pairs={{0,1},{1,2},{2,3},{4,5},{5,6},{6,7},{8,9},{9,10},{10,11},{12,13},{... | collective-permute-start | bytes 9224 | tf_op jit(solution)/shard_map/ppermute | solution.py:28
  18.3 4.3 %collective-permute-start.3 = (bf16[12,128]{1,0:T(8,128)(2,1)S(1)}, bf16[12,128]{1,0:T(8,128)(2,1)S(1)}, u32[]{:S(2)}, u32[]{:S(2)}) collective-permute-start(bf16[12,128]{1,0:T(8,128)(2,1)S(1)} %get-tuple-element.71), channel_id=1, source_target_pairs={{1,0},{2,1},{3,2},{5,4},{6,5},{7,6},{9,8},{10,9},{11,10},{13,12},{... | collective-permute-start | bytes 9224 | tf_op jit(solution)/shard_map/ppermute | solution.py:31
  22.6 3.8 %collective-permute-start.4 = (bf16[12,768]{1,0:T(8,128)(2,1)S(1)}, bf16[12,768]{1,0:T(8,128)(2,1)S(1)}, u32[]{:S(2)}, u32[]{:S(2)}) collective-permute-start(bf16[12,768]{1,0:T(8,128)(2,1)S(1)} %pad_maximum_fusion), channel_id=1, source_target_pairs={{0,4},{4,0},{8,12},{12,8},{16,20},{20,16},{24,28},{28,24},{1,5},{5... | collective-permute-start | bytes 55304 | tf_op jit(solution)/shard_map/ppermute | solution.py:15
  26.5 4.2 %collective-permute-start.5 = (bf16[24,768]{1,0:T(8,128)(2,1)S(1)}, bf16[24,768]{1,0:T(8,128)(2,1)S(1)}, u32[]{:S(2)}, u32[]{:S(2)}) collective-permute-start(bf16[24,768]{1,0:T(8,128)(2,1)S(1)} %maximum_select_fusion.2), channel_id=1, source_target_pairs={{0,8},{4,12},{8,0},{12,4},{16,24},{20,28},{24,16},{28,20},{1,9},{5... | collective-permute-start | bytes 110600 | tf_op jit(solution)/shard_map/ppermute | solution.py:15
  30.7 23.3 %collective-permute-start.6 = (bf16[48,768]{1,0:T(8,128)(2,1)S(1)}, bf16[48,768]{1,0:T(8,128)(2,1)S(1)}, u32[]{:S(2)}, u32[]{:S(2)}) collective-permute-start(bf16[48,768]{1,0:T(8,128)(2,1)S(1)} %maximum_select_fusion.1), channel_id=1, source_target_pairs={{0,16},{4,20},{8,24},{12,28},{16,0},{20,4},{24,8},{28,12},{1,17},{... | collective-permute-start | bytes 221192 | tf_op jit(solution)/shard_map/ppermute | solution.py:15
  49.8 2.8 %slice-start = ((bf16[12,196864]{1,0:T(8,128)(2,1)}), bf16[12,196608]{1,0:T(8,128)(2,1)S(1)}, s32[]{:S(2)}) async-start(bf16[12,196864]{1,0:T(8,128)(2,1)} %tile.10), calls=%async_computation | async-start | bytes 12582912 | tf_op jit(solution)/shard_map/slice | solution.py:57
